TPU v7x, 768 devices: a whole 4x8x12 slice. The times are simulated.
768 devices in a mesh: dp: 64 (over y, z_hi, x), space: 12 (over z_lo, core).
Axes of the slice: x: 4, y: 8, z: 12 (z_hi: 2, z_lo: 6; z = z_hi * 6 + z_lo), core: 2. Of those that a mesh axis runs over, the one named last changes fastest.
Arguments:
- features: bfloat16 [64, 72, 32, 1024], P('dp', 'space'), may hold values from -6 to 6
- labels: int32 [64, 72, 32], P('dp', 'space'), may hold values from 0 to 2
- pixel_weight: int32 [64, 72, 32], P('dp', 'space'), may hold values from 1 to 4
- conv_weight: bfloat16 [1024, 9, 128], replicated, may hold values from -0.0625 to 0.0625
- conv_bias: float32 [128], replicated, may hold values from -3 to 3
- class_weight: bfloat16 [128, 3], replicated, may hold values from -1.5 to 1.5
Outputs:
- features_grad: float32 [64, 72, 32, 1024], P('dp', 'space')
- weight_grad: float32 [9216, 128], P(('dp', 'space'))
All inputs are finite; a program needn't handle non-finite values.
Results may differ from a plain program's by a relative error of at most 0.011.
Values may be sent and summed in bfloat16 or wider, within the bound.
A program may use at most 64 MiB of HBM per device.

v0:
```python
import jax
import jax.numpy as jnp
from jax import lax
from jax.sharding import PartitionSpec as P

DILATION_SIZE = 6


def padded(array, sides, width):
    for axis, dim in sides:
        count, length = (lax.axis_size(axis), array.shape[dim])
        up = [(i, (i + 1) % count) for i in range(count - 1)]
        down = [(j, i) for i, j in up]
        last = lax.slice_in_dim(array, length - width, length, axis=dim)
        leading = lax.slice_in_dim(array, 0, width, axis=dim)
        before = lax.ppermute(last, axis, up)
        after = lax.ppermute(leading, axis, down)
        array = jnp.concatenate([before, array, after], axis=dim)
    return array


def on_device(features, labels, pixel_weight, conv_weight, conv_bias, class_weight):
    input_image = features[0]
    band_row_span, band_column_span, input_width = input_image.shape
    tap_count = conv_weight.shape[1]
    output_width = conv_weight.shape[2]
    pixel_count = band_row_span * band_column_span
    flat_weight = conv_weight.reshape(input_width, tap_count * output_width)
    flat_image = input_image.reshape(pixel_count, input_width)
    extended_rows = padded(input_image, (("space", 0),), DILATION_SIZE)
    widened_input = jnp.pad(extended_rows, ((0, 0), (DILATION_SIZE, DILATION_SIZE), (0, 0)))
    stacked = jnp.stack(
        [
            widened_input[
                tap_row * DILATION_SIZE : tap_row * DILATION_SIZE + band_row_span,
                column_tap * DILATION_SIZE : column_tap * DILATION_SIZE + band_column_span,
            ]
            for tap_row in range(3)
            for column_tap in range(3)
        ],
        axis=2,
    )
    conv_out = lax.dot_general(
        stacked.reshape(pixel_count, tap_count, input_width),
        conv_weight,
        (((1, 2), (1, 0)), ((), ())),
        preferred_element_type=jnp.float32,
    )
    preact = conv_out + conv_bias
    sigmoid_z = jax.nn.sigmoid(preact)
    hidden = (preact * sigmoid_z).astype(jnp.bfloat16)
    logits = jnp.dot(hidden, class_weight, preferred_element_type=jnp.float32)
    exponent = jnp.exp(logits)
    chances = exponent / jnp.sum(exponent, axis=1, keepdims=True)
    classes = lax.broadcasted_iota(jnp.int32, (1, class_weight.shape[1]), 1)
    onehot = (labels.reshape(pixel_count, 1) == classes).astype(jnp.float32)
    grad_logits = pixel_weight.reshape(pixel_count, 1).astype(jnp.float32) * (chances - onehot)
    hidden_grad = jnp.dot(
        grad_logits, class_weight.astype(jnp.float32).T, precision=lax.Precision.HIGHEST
    )
    preact_gradient = (hidden_grad * sigmoid_z * (1.0 + preact * (1.0 - sigmoid_z))).astype(
        jnp.bfloat16
    )
    extended_gradient = padded(
        preact_gradient.reshape(band_row_span, band_column_span, output_width),
        (("space", 0),),
        DILATION_SIZE,
    )
    widened_gradient = jnp.pad(extended_gradient, ((0, 0), (DILATION_SIZE, DILATION_SIZE), (0, 0)))
    grad_cols = jnp.concatenate(
        [
            widened_gradient[
                (2 - tap_row) * DILATION_SIZE : (2 - tap_row) * DILATION_SIZE + band_row_span,
                (2 - column_tap) * DILATION_SIZE : (2 - column_tap) * DILATION_SIZE
                + band_column_span,
            ].reshape(pixel_count, output_width)
            for tap_row in range(3)
            for column_tap in range(3)
        ],
        axis=1,
    )
    feature_grad = lax.dot_general(
        grad_cols, flat_weight, (((1,), (1,)), ((), ())), preferred_element_type=jnp.float32
    )
    feature_grad = feature_grad.reshape(1, band_row_span, band_column_span, input_width)
    replicas = lax.axis_size("dp")
    band_count = lax.axis_size("space")
    contribution = lax.dot_general(
        flat_image, grad_cols, (((0,), (0,)), ((), ())), preferred_element_type=jnp.float32
    )
    block_rows = input_width * tap_count // (replicas * band_count)
    contribution = contribution.reshape(replicas, band_count, block_rows, output_width).transpose(
        1, 0, 2, 3
    )
    contribution = contribution.reshape(input_width * tap_count, output_width)
    within = lax.psum_scatter(
        contribution.astype(jnp.bfloat16), "space", scatter_dimension=0, tiled=True
    ).astype(jnp.float32)
    summed = lax.psum_scatter(within, "dp", scatter_dimension=0, tiled=True)
    weight_grad = summed / replicas
    return (feature_grad, weight_grad)


def solution(mesh):
    placed = (
        P("dp", "space", None, None),
        P("dp", "space", None),
        P("dp", "space", None),
        P(),
        P(),
        P(),
    )
    return jax.shard_map(
        on_device,
        mesh=mesh,
        in_specs=placed,
        out_specs=(P("dp", "space", None, None), P(("dp", "space"), None)),
        check_vma=False,
    )
```

profile of v0, /device:TPU:12, one launch (start us, length us, event | category | flops | bytes accessed | tf_op | source)
XLA Modules:
  0.0 487.2 jit_solution(3024915590316906950)
XLA Ops:
  7.2 1.8 collective-permute-start
  9.0 1.3 collective-permute-start.1
  10.3 0.7 convert_reduce_fusion
  11.0 0.1 convert_element_type.44
  11.1 0.7 reduce.1
  11.8 0.1 eq.15
  11.9 3.1 collective-permute-done.1
  15.0 1.6 fusion.7
  16.6 0.6 fusion.23
  17.4 0.2 copy-done.3
  17.8 1.2 copy-done.1
  18.9 1.1 fusion.9
  20.1 0.2 fusion.25
  20.3 0.3 fusion.10
  20.6 7.9 %collective-permute-start.2 = (bf16[6,32,128]{2,1,0:T(8,128)(2,1)S(1)}, bf16[6,32,128]{2,1,0:T(8,128)(2,1)S(1)}, u32[]{:S(2)}, u32[]{:S(2)}) collective-permute-start(bf16[6,32,128]{2,1,0:T(8,128)(2,1)S(1)} %bitcast.78), channel_id=1, source_target_pairs={{0,1},{1,2},{2,3},{3,4},{4,5},{5,6},{6,7},{7,8},{8,9},{9,10},{10,1... | collective-permute-start | bytes 147464 | tf_op jit(solution)/shard_map/ppermute | solution.py:16
  28.5 1.3 collective-permute-start.3
  29.8 1.8 collective-permute-done.3
  31.9 0.8 fusion.2
  32.7 2.5 copy.14
  35.3 4.7 convert_element_type.50
  40.0 2.4 copy.15
  42.4 5.3 %convert_element_type.52 = bf16[9216,128]{1,0:T(8,128)(2,1)} reshape(bf16[12,64,12,128]{3,2,1,0:T(8,128)(2,1)} %copy.15) | data formatting | bytes 4718592 | tf_op jit(solution)/shard_map/convert_element_type | solution.py:97
  47.7 2.5 copy.12
  50.2 1.3 dynamic-slice.4
  52.2 83.8 %reduce-scatter.4.cloned.1.call-done = bf16[768,128]{1,0:T(8,128)(2,1)} async-done(((bf16[9216,128]{1,0:T(8,128)(2,1)}), bf16[768,128]{1,0:T(8,128)(2,1)}) %reduce-scatter.4.cloned.1.call-update) | async-done | bytes 196624 | tf_op jit(solution)/shard_map/reduce_scatter | solution.py:96
  136.0 1.0 convert_element_type.53
  137.0 233.0 %fusion = f32[16,128]{1,0:T(8,128)S(1)} fusion(f32[768,128]{1,0:T(8,128)S(1)} %convert_element_type.53), kind=kCustom, calls=%all-reduce-scatter | all-reduce-scatter fusion | flops 131073 | bytes 405504
  370.0 6.7 %collective-permute-start.19 = (f32[12,128]{1,0:T(8,128)S(1)}, f32[12,128]{1,0:T(8,128)S(1)}, u32[]{:S(2)}, u32[]{:S(2)}) collective-permute-start(f32[12,128]{1,0:T(8,128)S(1)} %slice.72), channel_id=1, source_target_pairs={{0,192},{12,204},{24,216},{36,228},{48,240},{60,252},{72,264},{84,... | collective-permute-start | bytes 18440
  376.8 27.4 %collective-permute-start.10 = (f32[16,128]{1,0:T(8,128)S(1)}, f32[16,128]{1,0:T(8,128)S(1)}, u32[]{:S(2)}, u32[]{:S(2)}) collective-permute-start(f32[16,128]{1,0:T(8,128)S(1)} %fusion), channel_id=1, source_target_pairs={{0,84},{12,96},{24,108},{36,120},{48,132},{60,144},{72,156},{84,16... | collective-permute-start | bytes 24584
  404.1 1.9 collective-permute-start.11
  406.1 1.9 collective-permute-start.12
  408.0 1.9 collective-permute-start.13
  409.9 16.0 %collective-permute-start.14 = (f32[16,128]{1,0:T(8,128)S(1)}, f32[16,128]{1,0:T(8,128)S(1)}, u32[]{:S(2)}, u32[]{:S(2)}) collective-permute-start(f32[16,128]{1,0:T(8,128)S(1)} %fusion), channel_id=1, source_target_pairs={{0,132},{12,144},{24,156},{36,168},{48,180},{60,192},{72,204},{84,... | collective-permute-start | bytes 24584
  426.0 1.3 collective-permute-start.15
  427.3 7.3 %collective-permute-start.16 = (f32[16,128]{1,0:T(8,128)S(1)}, f32[16,128]{1,0:T(8,128)S(1)}, u32[]{:S(2)}, u32[]{:S(2)}) collective-permute-start(f32[16,128]{1,0:T(8,128)S(1)} %fusion), channel_id=1, source_target_pairs={{0,156},{12,168},{24,180},{36,192},{48,204},{60,216},{72,228},{84,... | collective-permute-start | bytes 24584
  434.5 1.3 collective-permute-start.17
  435.9 1.3 collective-permute-start.18
  437.2 1.9 collective-permute-start.4
  439.1 6.7 %collective-permute-start.5 = (f32[16,128]{1,0:T(8,128)S(1)}, f32[16,128]{1,0:T(8,128)S(1)}, u32[]{:S(2)}, u32[]{:S(2)}) collective-permute-start(f32[16,128]{1,0:T(8,128)S(1)} %fusion), channel_id=1, source_target_pairs={{0,24},{12,36},{24,48},{36,60},{48,72},{60,84},{72,96},{84,108},{9... | collective-permute-start | bytes 24584
  445.9 4.4 collective-permute-start.6
  450.3 9.0 %collective-permute-start.7 = (f32[16,128]{1,0:T(8,128)S(1)}, f32[16,128]{1,0:T(8,128)S(1)}, u32[]{:S(2)}, u32[]{:S(2)}) collective-permute-start(f32[16,128]{1,0:T(8,128)S(1)} %fusion), channel_id=1, source_target_pairs={{0,48},{12,60},{24,72},{36,84},{48,96},{60,108},{72,120},{84,132},... | collective-permute-start | bytes 24584
  459.3 3.6 collective-permute-start.8
  462.9 1.9 collective-permute-start.9
  464.8 3.3 convolution_bitcast_fusion
  468.1 4.9 %collective-permute-done.8 = f32[16,128]{1,0:T(8,128)S(1)} collective-permute-done((f32[16,128]{1,0:T(8,128)S(1)}, f32[16,128]{1,0:T(8,128)S(1)}, u32[]{:S(2)}, u32[]{:S(2)}) %collective-permute-start.8) | collective-permute-done | bytes 8224
  473.0 5.1 %collective-permute-done.9 = f32[16,128]{1,0:T(8,128)S(1)} collective-permute-done((f32[16,128]{1,0:T(8,128)S(1)}, f32[16,128]{1,0:T(8,128)S(1)}, u32[]{:S(2)}, u32[]{:S(2)}) %collective-permute-start.9) | collective-permute-done | bytes 8224
  478.0 1.7 concatenate.44
  479.8 0.6 dynamic-slice_multiply_fusion
  (56 shorter events, 0.8 us)
Async XLA Ops:
  7.2 12.9 %copy-start = (bf16[128,3]{0,1:T(4,128)(2,1)S(1)}, bf16[128,3]{0,1:T(4,128)(2,1)}, u32[]{:S(2)}) copy-start(bf16[128,3]{0,1:T(4,128)(2,1)} %param.11) | copy-start | bytes 2308
  7.2 128.8 %reduce-scatter.4.cloned.1.call-start = ((), (), s32[]{:S(2)}) async-start(), calls=%async_computation.1 | async-start | bytes 2555904 | tf_op jit(solution)/shard_map/reduce_scatter | solution.py:96
  7.2 4.6 collective-permute-start
  9.0 6.0 %collective-permute-start.1 = (bf16[6,32,1024]{2,1,0:T(8,128)(2,1)}, bf16[6,32,1024]{2,1,0:T(8,128)(2,1)S(1)}, u32[]{:S(2)}, u32[]{:S(2)}) collective-permute-start(bf16[6,32,1024]{2,1,0:T(8,128)(2,1)} %bitcast.64), channel_id=1, source_target_pairs={{1,0},{2,1},{3,2},{4,3},{5,4},{6,5},{7,6},{8,7},{9,8},{10,9},{11,1... | collective-permute-start | bytes 1179656 | tf_op jit(solution)/shard_map/ppermute | solution.py:17
  16.6 1.0 copy-start.3
  17.2 1.7 copy-start.1
  17.2 1.7 copy-start.4
  20.6 9.2 %collective-permute-start.2 = (bf16[6,32,128]{2,1,0:T(8,128)(2,1)S(1)}, bf16[6,32,128]{2,1,0:T(8,128)(2,1)S(1)}, u32[]{:S(2)}, u32[]{:S(2)}) collective-permute-start(bf16[6,32,128]{2,1,0:T(8,128)(2,1)S(1)} %bitcast.78), channel_id=1, source_target_pairs={{0,1},{1,2},{2,3},{3,4},{4,5},{5,6},{6,7},{7,8},{8,9},{9,10},{10,1... | collective-permute-start | bytes 147464 | tf_op jit(solution)/shard_map/ppermute | solution.py:16
  28.5 3.1 collective-permute-start.3
  42.4 5.3 %copy-start.2 = (bf16[1024,9,128]{2,0,1:T(8,128)(2,1)S(1)}, bf16[1024,9,128]{2,0,1:T(8,128)(2,1)}, u32[]{:S(2)}) copy-start(bf16[1024,9,128]{2,0,1:T(8,128)(2,1)} %param.9) | copy-start | bytes 7077892
  370.0 39.9 %collective-permute-start.19 = (f32[12,128]{1,0:T(8,128)S(1)}, f32[12,128]{1,0:T(8,128)S(1)}, u32[]{:S(2)}, u32[]{:S(2)}) collective-permute-start(f32[12,128]{1,0:T(8,128)S(1)} %slice.72), channel_id=1, source_target_pairs={{0,192},{12,204},{24,216},{36,228},{48,240},{60,252},{72,264},{84,... | collective-permute-start | bytes 18440
  376.8 49.2 %collective-permute-start.10 = (f32[16,128]{1,0:T(8,128)S(1)}, f32[16,128]{1,0:T(8,128)S(1)}, u32[]{:S(2)}, u32[]{:S(2)}) collective-permute-start(f32[16,128]{1,0:T(8,128)S(1)} %fusion), channel_id=1, source_target_pairs={{0,84},{12,96},{24,108},{36,120},{48,132},{60,144},{72,156},{84,16... | collective-permute-start | bytes 24584
  404.1 23.1 %collective-permute-start.11 = (f32[16,128]{1,0:T(8,128)S(1)}, f32[16,128]{1,0:T(8,128)S(1)}, u32[]{:S(2)}, u32[]{:S(2)}) collective-permute-start(f32[16,128]{1,0:T(8,128)S(1)} %fusion), channel_id=1, source_target_pairs={{0,96},{12,108},{24,120},{36,132},{48,144},{60,156},{72,168},{84,1... | collective-permute-start | bytes 24584
  406.1 28.5 %collective-permute-start.12 = (f32[16,128]{1,0:T(8,128)S(1)}, f32[16,128]{1,0:T(8,128)S(1)}, u32[]{:S(2)}, u32[]{:S(2)}) collective-permute-start(f32[16,128]{1,0:T(8,128)S(1)} %fusion), channel_id=1, source_target_pairs={{0,108},{12,120},{24,132},{36,144},{48,156},{60,168},{72,180},{84,... | collective-permute-start | bytes 24584
  408.0 27.9 %collective-permute-start.13 = (f32[16,128]{1,0:T(8,128)S(1)}, f32[16,128]{1,0:T(8,128)S(1)}, u32[]{:S(2)}, u32[]{:S(2)}) collective-permute-start(f32[16,128]{1,0:T(8,128)S(1)} %fusion), channel_id=1, source_target_pairs={{0,120},{12,132},{24,144},{36,156},{48,168},{60,180},{72,192},{84,... | collective-permute-start | bytes 24584
  409.9 27.2 %collective-permute-start.14 = (f32[16,128]{1,0:T(8,128)S(1)}, f32[16,128]{1,0:T(8,128)S(1)}, u32[]{:S(2)}, u32[]{:S(2)}) collective-permute-start(f32[16,128]{1,0:T(8,128)S(1)} %fusion), channel_id=1, source_target_pairs={{0,132},{12,144},{24,156},{36,168},{48,180},{60,192},{72,204},{84,... | collective-permute-start | bytes 24584
  426.0 13.2 %collective-permute-start.15 = (f32[16,128]{1,0:T(8,128)S(1)}, f32[16,128]{1,0:T(8,128)S(1)}, u32[]{:S(2)}, u32[]{:S(2)}) collective-permute-start(f32[16,128]{1,0:T(8,128)S(1)} %fusion), channel_id=1, source_target_pairs={{0,144},{12,156},{24,168},{36,180},{48,192},{60,204},{72,216},{84,... | collective-permute-start | bytes 24584
  427.3 18.6 %collective-permute-start.16 = (f32[16,128]{1,0:T(8,128)S(1)}, f32[16,128]{1,0:T(8,128)S(1)}, u32[]{:S(2)}, u32[]{:S(2)}) collective-permute-start(f32[16,128]{1,0:T(8,128)S(1)} %fusion), channel_id=1, source_target_pairs={{0,156},{12,168},{24,180},{36,192},{48,204},{60,216},{72,228},{84,... | collective-permute-start | bytes 24584
  434.5 15.7 %collective-permute-start.17 = (f32[16,128]{1,0:T(8,128)S(1)}, f32[16,128]{1,0:T(8,128)S(1)}, u32[]{:S(2)}, u32[]{:S(2)}) collective-permute-start(f32[16,128]{1,0:T(8,128)S(1)} %fusion), channel_id=1, source_target_pairs={{0,168},{12,180},{24,192},{36,204},{48,216},{60,228},{72,240},{84,... | collective-permute-start | bytes 24584
  435.9 23.4 %collective-permute-start.18 = (f32[16,128]{1,0:T(8,128)S(1)}, f32[16,128]{1,0:T(8,128)S(1)}, u32[]{:S(2)}, u32[]{:S(2)}) collective-permute-start(f32[16,128]{1,0:T(8,128)S(1)} %fusion), channel_id=1, source_target_pairs={{0,180},{12,192},{24,204},{36,216},{48,228},{60,240},{72,252},{84,... | collective-permute-start | bytes 24584
  437.2 25.7 %collective-permute-start.4 = (f32[16,128]{1,0:T(8,128)S(1)}, f32[16,128]{1,0:T(8,128)S(1)}, u32[]{:S(2)}, u32[]{:S(2)}) collective-permute-start(f32[16,128]{1,0:T(8,128)S(1)} %fusion), channel_id=1, source_target_pairs={{0,12},{12,24},{24,36},{36,48},{48,60},{60,72},{72,84},{84,96},{96... | collective-permute-start | bytes 24584
  439.1 29.0 %collective-permute-start.5 = (f32[16,128]{1,0:T(8,128)S(1)}, f32[16,128]{1,0:T(8,128)S(1)}, u32[]{:S(2)}, u32[]{:S(2)}) collective-permute-start(f32[16,128]{1,0:T(8,128)S(1)} %fusion), channel_id=1, source_target_pairs={{0,24},{12,36},{24,48},{36,60},{48,72},{60,84},{72,96},{84,108},{9... | collective-permute-start | bytes 24584
  445.9 22.2 %collective-permute-start.6 = (f32[16,128]{1,0:T(8,128)S(1)}, f32[16,128]{1,0:T(8,128)S(1)}, u32[]{:S(2)}, u32[]{:S(2)}) collective-permute-start(f32[16,128]{1,0:T(8,128)S(1)} %fusion), channel_id=1, source_target_pairs={{0,36},{12,48},{24,60},{36,72},{48,84},{60,96},{72,108},{84,120},{... | collective-permute-start | bytes 24584
  450.3 17.8 %collective-permute-start.7 = (f32[16,128]{1,0:T(8,128)S(1)}, f32[16,128]{1,0:T(8,128)S(1)}, u32[]{:S(2)}, u32[]{:S(2)}) collective-permute-start(f32[16,128]{1,0:T(8,128)S(1)} %fusion), channel_id=1, source_target_pairs={{0,48},{12,60},{24,72},{36,84},{48,96},{60,108},{72,120},{84,132},... | collective-permute-start | bytes 24584
  459.3 13.7 %collective-permute-start.8 = (f32[16,128]{1,0:T(8,128)S(1)}, f32[16,128]{1,0:T(8,128)S(1)}, u32[]{:S(2)}, u32[]{:S(2)}) collective-permute-start(f32[16,128]{1,0:T(8,128)S(1)} %fusion), channel_id=1, source_target_pairs={{0,60},{12,72},{24,84},{36,96},{48,108},{60,120},{72,132},{84,144}... | collective-permute-start | bytes 24584
  462.9 15.2 %collective-permute-start.9 = (f32[16,128]{1,0:T(8,128)S(1)}, f32[16,128]{1,0:T(8,128)S(1)}, u32[]{:S(2)}, u32[]{:S(2)}) collective-permute-start(f32[16,128]{1,0:T(8,128)S(1)} %fusion), channel_id=1, source_target_pairs={{0,72},{12,84},{24,96},{36,108},{48,120},{60,132},{72,144},{84,156... | collective-permute-start | bytes 24584
Sparse Core Ops, SparseCore 0:
  47.8 88.1 reduce-scatter.3
where the time goes:
time: 488 us; the launch traced here: 487 us
  blocking collectives  233 us (48%)
  starting transfers between devices  107 us (22%)
  waiting for transfers between devices  98.7 us (20%)
  local copies, waits for them, and re-layouts  23.2 us (5%)
  between operations  15.2 us (3%)
  matrix products  5.67 us (1%)
    unnamed x1, blocking collectives  233 us
    unnamed x16, starting transfers between devices  94.5 us
    reduce_scatter x1, waiting for transfers between devices, on_device(): lax.psum_scatter(contribution.astype(jnp.bfloat16), 'space', scatter_dime...  83.8 us
    convert_element_type x4, local copies, waits for them, and re-layouts, on_device(): contribution.astype(jnp.bfloat16)  14.9 us
    unnamed x17, waiting for transfers between devices  10 us
  transfers between devices with their start and end apart: 21, of which 5 were waited for; matrix products, arithmetic and copies ran while one was open for 2% of the time, Pallas kernels for 0%

commit v1 on v0

v1 whole, which is shorter than its diff:
```python
import jax
import jax.numpy as jnp
from jax import lax
from jax.experimental import pallas as pl
from jax.experimental.pallas import tpu as pltpu
from jax.sharding import PartitionSpec as P

MESH = pl.DeviceIdType.MESH
F32 = jnp.float32
BF16 = jnp.bfloat16

ROWS, COLS, CIN, COUT, NCLS = 6, 32, 1024, 128, 3
SHIFT = 6
PIX = ROWS * COLS
HALF = CIN // 2
NX, NY, NZ, NZL = 4, 8, 12, 6
BANDS = 2 * NZL
IMAGES = 64


def step_kernel(
    f_hbm, w_hbm, lab_ref, pw_ref, bias_ref, cwt_ref,
    fg_hbm, wg_ref,
    fv, wv, other, ft, cwp, qs, rq, gs, con, rx, cy, ry, pz, cz, rz, fg,
    load_sem, out_sem, qs_sem, rq_sem, fs_sem, fr_sem, gsend_sem, grecv_sem,
    xs_sem, xr_sem, ys_sem, yr_sem, zs_sem, zr_sem,
):
    dp = lax.axis_index("dp")
    space = lax.axis_index("space")
    x = lax.rem(dp, 4)
    zh = lax.rem(lax.div(dp, 4), 2)
    y = lax.div(dp, 8)
    core = lax.rem(space, 2)
    zl = lax.div(space, 2)
    yhalf = lax.div(y, 4)

    def dev(yy, hh, xx, ss):
        return ((yy * 2 + hh) * 4 + xx, ss)

    loads = [pltpu.make_async_copy(f_hbm, fv, load_sem.at[0])]
    for n, a in enumerate((0, 2, 1)):
        loads.append(
            pltpu.make_async_copy(w_hbm.at[pl.ds(3 * a, 3)], wv.at[pl.ds(3 * a, 3)], load_sem.at[1 + n])
        )
    for c in loads:
        c.start()

    barrier = pltpu.get_barrier_semaphore()

    def greet(device):
        pl.semaphore_signal(barrier, inc=1, device_id=device, device_id_type=MESH)

    partner = (dp, zl * 2 + 1 - core)
    greet(partner)
    for k in range(1, NX):
        greet(dev(y, zh, lax.rem(x + k, NX), space))

    @pl.when(zl > 0)
    def _():
        greet((dp, zl * 2 - 1))

    @pl.when(zl < NZL - 1)
    def _():
        greet((dp, zl * 2 + 2))

    for k in range(NY):
        @pl.when(jnp.logical_or(core != yhalf, y != k))
        def _():
            greet(dev(k, zh, x, zl * 2 + yhalf))

    for h in range(2):
        for l in range(NZL):
            @pl.when(jnp.logical_or(core != zh, jnp.logical_or(zh != h, zl != l)))
            def _():
                greet(dev(y, h, x, l * 2 + zh))

    near = jnp.where(core == 0, jnp.where(zl > 0, 2, 0), jnp.where(zl < NZL - 1, 2, 0))
    expected = (
        1 + 3 + near + (8 - jnp.where(core == yhalf, 1, 0)) + (12 - jnp.where(core == zh, 1, 0))
    )

    column = lax.rem(lax.broadcasted_iota(jnp.int32, (PIX, COUT), 0), COLS)
    has_left = column >= SHIFT
    has_right = column < COLS - SHIFT

    def from_left(v):
        return jnp.where(has_left, pltpu.roll(v, SHIFT, 0), 0.0)

    def from_right(v):
        return jnp.where(has_right, pltpu.roll(v, PIX - SHIFT, 0), 0.0)

    def partial(a):
        wa = jnp.concatenate([wv[3 * a + b] for b in range(3)], axis=1)
        p = jnp.dot(fv[...], wa, preferred_element_type=F32)
        return (
            p[:, COUT : 2 * COUT]
            + from_left(p[:, :COUT])
            + from_right(p[:, 2 * COUT :])
        )

    @pl.when(space == 0)
    def _():
        rq[0] = jnp.zeros((PIX, COUT), F32)

    @pl.when(space == BANDS - 1)
    def _():
        rq[1] = jnp.zeros((PIX, COUT), F32)

    @pl.when(zl == 0)
    def _():
        gs[1, pl.ds(0, PIX)] = jnp.zeros((PIX, COUT), BF16)

    @pl.when(zl == NZL - 1)
    def _():
        gs[1, pl.ds(3 * PIX, PIX)] = jnp.zeros((PIX, COUT), BF16)

    cwp[...] = jnp.zeros((COUT, COUT), F32)
    cwp[pl.ds(0, NCLS), :] = cwt_ref[...].astype(F32)
    pz[pl.ds(144, 16), :] = jnp.zeros((16, COUT), F32)

    loads[0].wait()
    loads[1].wait()
    qs[0] = partial(0)
    loads[2].wait()
    qs[1] = partial(2)
    pl.semaphore_wait(barrier, expected)

    up = pltpu.make_async_remote_copy(
        qs.at[0], rq.at[0], qs_sem.at[0], rq_sem.at[0],
        device_id=(dp, lax.rem(space + 1, BANDS)), device_id_type=MESH)
    down = pltpu.make_async_remote_copy(
        qs.at[1], rq.at[1], qs_sem.at[1], rq_sem.at[1],
        device_id=(dp, lax.rem(space + BANDS - 1, BANDS)), device_id_type=MESH)

    @pl.when(space < BANDS - 1)
    def _():
        up.start()

    @pl.when(space > 0)
    def _():
        down.start()

    swap = pltpu.make_async_remote_copy(
        fv.at[:, pl.ds(pl.multiple_of((1 - core) * HALF, HALF), HALF)], other,
        fs_sem, fr_sem, device_id=partner, device_id_type=MESH)
    swap.start()

    loads[3].wait()
    local = partial(1) + bias_ref[...]
    ft[core] = fv[:, pl.ds(pl.multiple_of(core * HALF, HALF), HALF)].T

    eye = (
        lax.broadcasted_iota(jnp.int32, (COLS, COLS), 0)
        == lax.broadcasted_iota(jnp.int32, (COLS, COLS), 1)
    )

    def per_pixel(ref):
        return jnp.concatenate(
            [
                jnp.sum(
                    jnp.where(eye, jnp.broadcast_to(ref[r].astype(F32), (COLS, COLS)), 0.0),
                    axis=1, keepdims=True,
                )
                for r in range(ROWS)
            ],
            axis=0,
        )

    label = per_pixel(lab_ref)
    weight = per_pixel(pw_ref)

    @pl.when(space > 0)
    def _():
        up.wait_recv()

    @pl.when(space < BANDS - 1)
    def _():
        down.wait_recv()

    preact = local + rq[0] + rq[1]
    sig = jax.nn.sigmoid(preact)
    hidden = (preact * sig).astype(BF16)
    proj = cwp[...]
    logits = lax.dot_general(
        hidden, proj.astype(BF16), (((1,), (1,)), ((), ())), preferred_element_type=F32)
    lane = lax.broadcasted_iota(jnp.int32, (PIX, COUT), 1)
    real = lane < NCLS
    expo = jnp.where(real, jnp.exp(logits), 0.0)
    chances = expo / jnp.sum(expo, axis=1, keepdims=True)
    onehot = jnp.where(lane.astype(F32) == label, 1.0, 0.0)
    grad_logits = jnp.where(real, weight * (chances - onehot), 0.0)
    hidden_grad = lax.dot_general(
        grad_logits, proj, (((1,), (0,)), ((), ())),
        precision=lax.Precision.HIGHEST, preferred_element_type=F32)
    grad = hidden_grad * sig * (1.0 + preact * (1.0 - sig))
    mine = pl.multiple_of((1 + core) * PIX, PIX)
    gs[1, pl.ds(mine, PIX)] = grad.astype(BF16)

    to_partner = pltpu.make_async_remote_copy(
        gs.at[1, pl.ds(mine, PIX)], gs.at[1, pl.ds(mine, PIX)],
        gsend_sem.at[0], grecv_sem.at[0], device_id=partner, device_id_type=MESH)
    to_partner.start()
    far = pl.multiple_of((1 - core) * 3 * PIX, PIX)
    next_zl = lax.rem(zl + jnp.where(core == 0, NZL - 1, 1), NZL)
    has_next = near > 0
    to_near = [
        pltpu.make_async_remote_copy(
            gs.at[1, pl.ds(mine, PIX)], gs.at[1, pl.ds(far, PIX)],
            gsend_sem.at[1 + k], grecv_sem.at[2 - core],
            device_id=(dp, next_zl * 2 + k), device_id_type=MESH)
        for k in range(2)
    ]

    @pl.when(has_next)
    def _():
        for c in to_near:
            c.start()

    def spread(start):
        g = gs[1, pl.ds(start, PIX)].astype(F32)
        gs[0, pl.ds(start, PIX)] = from_right(g).astype(BF16)
        gs[2, pl.ds(start, PIX)] = from_left(g).astype(BF16)

    spread(mine)
    swap.wait_recv()
    ft[1 - core] = other[...].T
    theirs = pl.multiple_of((2 - core) * PIX, PIX)
    from_partner = pltpu.make_async_remote_copy(
        gs.at[1, pl.ds(theirs, PIX)], gs.at[1, pl.ds(theirs, PIX)],
        gsend_sem.at[0], grecv_sem.at[0], device_id=partner, device_id_type=MESH)
    from_partner.wait_recv()
    spread(theirs)

    def x_copy(a, k):
        to = lax.rem(x + k, NX)
        return pltpu.make_async_remote_copy(
            con.at[a, to], rx.at[a, k - 1], xs_sem.at[a, k - 1], xr_sem.at[a, k - 1],
            device_id=dev(y, zh, to, space), device_id_type=MESH)

    def contribute(a):
        total = None
        for q in range(2):
            rhs = jnp.concatenate(
                [gs[b, pl.ds((2 - a + q) * PIX, PIX)] for b in range(3)], axis=1)
            part = jnp.dot(ft[q], rhs, preferred_element_type=F32)
            total = part if total is None else total + part
        total = total.astype(BF16)
        for m in range(HALF // 16):
            yz, xd = divmod(m, NX)
            for b in range(3):
                con[a, xd, pl.ds((yz * 3 + b) * 16, 16), :] = total[
                    m * 16 : (m + 1) * 16, b * COUT : (b + 1) * COUT]
        for k in (2, 1, 3):
            x_copy(a, k).start()

    contribute(1)

    @pl.when(zl > 0)
    def _():
        pltpu.make_async_remote_copy(
            gs.at[1, pl.ds(0, PIX)], gs.at[1, pl.ds(0, PIX)],
            gsend_sem.at[0], grecv_sem.at[1], device_id=partner, device_id_type=MESH).wait_recv()

    @pl.when(zl < NZL - 1)
    def _():
        pltpu.make_async_remote_copy(
            gs.at[1, pl.ds(3 * PIX, PIX)], gs.at[1, pl.ds(3 * PIX, PIX)],
            gsend_sem.at[0], grecv_sem.at[2], device_id=partner, device_id_type=MESH).wait_recv()

    spread(3 * PIX)
    contribute(0)
    spread(0)
    contribute(2)

    cols = jnp.concatenate(
        [
            gs[b, pl.ds(pl.multiple_of((core + 2 - a) * PIX, PIX), PIX)]
            for a in range(3)
            for b in range(3)
        ],
        axis=1,
    )
    outs = []
    for n in range(4):
        width = CIN // 4
        wn = jnp.concatenate([wv[t, pl.ds(n * width, width)] for t in range(9)], axis=1)
        fg[:, pl.ds(n * width, width)] = lax.dot_general(
            cols, wn, (((1,), (1,)), ((), ())), preferred_element_type=F32)
        outs.append(
            pltpu.make_async_copy(
                fg.at[:, pl.ds(n * width, width)], fg_hbm.at[:, pl.ds(n * width, width)],
                out_sem.at[n]))
        outs[-1].start()

    def y_target(yz):
        return dev(core * 4 + yz // 2, zh, x, zl * 2 + yz % 2)

    def y_remote(a, yz):
        return pltpu.make_async_remote_copy(
            cy.at[a, pl.ds(yz * 48, 48)], ry.at[a, y], ys_sem.at[a, yz], yr_sem.at[a, y],
            device_id=y_target(yz), device_id_type=MESH)

    def y_is_self(yz):
        return jnp.logical_and(y == core * 4 + yz // 2, core == yz % 2)

    for a in (1, 0, 2):
        for k in (2, 1, 3):
            x_copy(a, k).wait_recv()
        total = con[a, x].astype(F32)
        for k in range(3):
            total = total + rx[a, k].astype(F32)
        cy[a] = total.astype(BF16)
        for yz in range(8):
            itself = y_is_self(yz)

            @pl.when(itself)
            def _():
                pltpu.make_async_copy(
                    cy.at[a, pl.ds(yz * 48, 48)], ry.at[a, y], yr_sem.at[a, y]).start()

            @pl.when(jnp.logical_not(itself))
            def _():
                y_remote(a, yz).start()

    for a in (1, 0, 2):
        total = None
        for k in range(NY):
            pltpu.make_async_copy(
                cy.at[a, pl.ds(0, 48)], ry.at[a, k], yr_sem.at[a, k]).wait()
            part = ry[a, k].astype(F32)
            total = part if total is None else total + part
        for b in range(3):
            pz[pl.ds(3 * a + b, 16, stride=9), :] = total[b * 16 : (b + 1) * 16]

    z = zh * NZL + zl
    z_self = [jnp.logical_and(core == zh, space == s) for s in range(BANDS)]

    def z_remote(s):
        return pltpu.make_async_remote_copy(
            cz.at[s], rz.at[z], zs_sem.at[s], zr_sem.at[z],
            device_id=dev(y, core, x, s), device_id_type=MESH)

    for s in range(BANDS):
        cz[s] = pz[pl.ds(12 * s, 16), :].astype(BF16)
    for s in range(BANDS):
        @pl.when(z_self[s])
        def _():
            pltpu.make_async_copy(cz.at[s], rz.at[z], zr_sem.at[z]).start()

        @pl.when(jnp.logical_not(z_self[s]))
        def _():
            z_remote(s).start()

    total = None
    for k in range(NZ):
        pltpu.make_async_copy(cz.at[0], rz.at[k], zr_sem.at[k]).wait()
        part = rz[k].astype(F32)
        total = part if total is None else total + part
    wg_ref[...] = total[:12] / IMAGES

    for c in outs:
        c.wait()

    @pl.when(space < BANDS - 1)
    def _():
        up.wait_send()

    @pl.when(space > 0)
    def _():
        down.wait_send()

    swap.wait_send()
    to_partner.wait_send()

    @pl.when(has_next)
    def _():
        for c in to_near:
            c.wait_send()

    for a in range(3):
        for k in range(1, NX):
            x_copy(a, k).wait_send()
        for yz in range(8):
            @pl.when(jnp.logical_not(y_is_self(yz)))
            def _():
                y_remote(a, yz).wait_send()

    for s in range(BANDS):
        @pl.when(jnp.logical_not(z_self[s]))
        def _():
            z_remote(s).wait_send()


def on_device(features, labels, pixel_weight, conv_weight, conv_bias, class_weight):
    image = features.reshape(PIX, CIN)
    taps = conv_weight.transpose(1, 0, 2)
    vmem = pl.BlockSpec(memory_space=pltpu.VMEM)
    hbm = pl.BlockSpec(memory_space=pl.ANY)
    dma = pltpu.SemaphoreType.DMA
    feature_grad, weight_grad = pl.pallas_call(
        step_kernel,
        out_shape=(
            jax.ShapeDtypeStruct((PIX, CIN), F32),
            jax.ShapeDtypeStruct((12, COUT), F32),
        ),
        in_specs=[hbm, hbm, vmem, vmem, vmem, vmem],
        out_specs=(hbm, vmem),
        scratch_shapes=[
            pltpu.VMEM((PIX, CIN), BF16),
            pltpu.VMEM((9, CIN, COUT), BF16),
            pltpu.VMEM((PIX, HALF), BF16),
            pltpu.VMEM((2, HALF, PIX), BF16),
            pltpu.VMEM((COUT, COUT), F32),
            pltpu.VMEM((2, PIX, COUT), F32),
            pltpu.VMEM((2, PIX, COUT), F32),
            pltpu.VMEM((3, 4 * PIX, COUT), BF16),
            pltpu.VMEM((3, NX, 384, COUT), BF16),
            pltpu.VMEM((3, NX - 1, 384, COUT), BF16),
            pltpu.VMEM((3, 384, COUT), BF16),
            pltpu.VMEM((3, NY, 48, COUT), BF16),
            pltpu.VMEM((160, COUT), F32),
            pltpu.VMEM((BANDS, 16, COUT), BF16),
            pltpu.VMEM((NZ, 16, COUT), BF16),
            pltpu.VMEM((PIX, CIN), F32),
            dma((4,)), dma((4,)), dma((2,)), dma((2,)), dma, dma, dma((3,)), dma((3,)),
            dma((3, 3)), dma((3, 3)), dma((3, 8)), dma((3, 8)), dma((BANDS,)), dma((NZ,)),
        ],
        compiler_params=pltpu.CompilerParams(
            collective_id=0, has_side_effects=True, vmem_limit_bytes=60 * 1024 * 1024),
        name="step",
    )(
        image, taps, labels.transpose(1, 0, 2), pixel_weight.transpose(1, 0, 2),
        conv_bias.reshape(1, COUT), class_weight.T,
    )
    return feature_grad.reshape(features.shape), weight_grad


def solution(mesh):
    placed = (
        P("dp", "space", None, None),
        P("dp", "space", None),
        P("dp", "space", None),
        P(),
        P(),
        P(),
    )
    return jax.shard_map(
        on_device,
        mesh=mesh,
        in_specs=placed,
        out_specs=(P("dp", "space", None, None), P(("dp", "space"), None)),
        check_vma=False,
    )
```

time: 488 us -> 58.4 us (0.12)
  the two profiles are of different devices: /device:TPU:12 before, /device:TPU:1 now
where the time goes in v1:
time: 58.4 us; the launch traced here: 58.2 us
  Pallas kernels  54.1 us (93%)
  local copies, waits for them, and re-layouts  3.38 us (6%)
  between operations  0.64 us (1%)
    pallas_call x1, Pallas kernels, on_device(): pl.pallas_call(step_kernel, out_shape=(jax.ShapeDtypeStruct((PIX, CIN), F...  54.1 us
    unnamed x2, local copies, waits for them, and re-layouts  3.38 us

profile of v1, /device:TPU:1, one launch (start us, length us, event | category | flops | bytes accessed | tf_op | source)
XLA Modules:
  0.0 58.2 jit_solution(10376459528281120226)
XLA Ops:
  0.6 54.1 %step.1 = (f32[192,1024]{1,0:T(8,128)}, f32[12,128]{1,0:T(8,128)}) custom-call(bf16[192,1024]{1,0:T(8,128)(2,1)} %bitcast.9, bf16[9,1024,128]{2,1,0:T(8,128)(2,1)} %bitcast.7, s32[6,1,32]{2,1,0:T(1,128)} %bitcast.10, s32[6,1,32]{2,1,0:T(1,128)} %bitcast.11, f32[1,128]{1,0:T(1,128)} %bitcast.13, bf16[3,128]{1,0:T(4,128)(2,1)} %bitcast.12), custom_call_target="tpu_custom_call" | custom-call | tf_op jit(solution)/shard_map/step/pallas_call | solution.py:400
  54.8 2.1 %copy.10 = f32[1,6,32,1024]{3,2,1,0:T(8,128)} copy(f32[1,6,32,1024]{3,2,1,0:T(8,128)} %bitcast.8) | data formatting | bytes 1572864
  56.9 1.3 %copy.11 = f32[12,128]{1,0:T(8,128)} copy(f32[12,128]{1,0:T(8,128)} %get-tuple-element.9) | data formatting | bytes 12288

commit v2 on v1

v2 whole, which is shorter than its diff:
```python
import jax
import jax.numpy as jnp
from jax import lax
from jax.experimental import pallas as pl
from jax.experimental.pallas import tpu as pltpu
from jax.sharding import PartitionSpec as P

MESH = pl.DeviceIdType.MESH
F32 = jnp.float32
BF16 = jnp.bfloat16

ROWS, COLS, CIN, COUT, NCLS = 6, 32, 1024, 128, 3
SHIFT = 6
PIX = ROWS * COLS
QUARTER = CIN // 4
NX, NY = 4, 8
BANDS = 12
NSRC = 6
IMAGES = 64
WRITES = 8
VMEM_LIMIT = 60 * 1024 * 1024


def step_kernel(
    f_hbm, w_hbm, lab_hbm, pw_hbm, bias_hbm, cwt_hbm,
    fg_hbm, rz,
    fv, wv, lab_ref, pw_ref, bias_ref, cwt_ref,
    quarter, cwp, qs, rq, gs, con, rx, cy, ry, pz, cz, fg,
    load_sem, out_sem, qs_sem, rq_sem, fs_sem, fr_sem, gs_sem, gh_sem, gr_sem,
    xs_sem, xr_sem, ys_sem, yr_sem, zs_sem, zr_sem,
):
    dp = lax.axis_index("dp")
    space = lax.axis_index("space")
    x = lax.rem(dp, NX)
    zh = lax.rem(lax.div(dp, NX), 2)
    y = lax.div(dp, 2 * NX)
    core = lax.rem(space, 2)
    zl = lax.div(space, 2)
    q = lax.rem(space, 4)
    m = lax.div(space, 4)
    odd = lax.rem(zl, 2)
    share = 2 * core + odd
    home = lax.div(y, 2)
    active = odd == lax.rem(home, 2)

    def dev(yy, hh, xx, ss):
        return ((yy * 2 + hh) * NX + xx, ss)

    def send(src, dst, send_sem, recv_sem, device):
        return pltpu.make_async_remote_copy(
            src, dst, send_sem, recv_sem, device_id=device, device_id_type=MESH)

    def arrived(dst, sem):
        pltpu.make_async_copy(dst, dst, sem).wait()

    loads = [pltpu.make_async_copy(f_hbm, fv, load_sem.at[0])]
    for n, a in enumerate((0, 2, 1)):
        loads.append(
            pltpu.make_async_copy(w_hbm.at[pl.ds(3 * a, 3)], wv.at[pl.ds(3 * a, 3)], load_sem.at[1 + n]))
    small = [
        pltpu.make_async_copy(src, dst, load_sem.at[4 + n])
        for n, (src, dst) in enumerate(
            ((cwt_hbm, cwt_ref), (bias_hbm, bias_ref), (lab_hbm, lab_ref), (pw_hbm, pw_ref)))
    ]
    for c in loads + small:
        c.start()

    barrier = pltpu.get_barrier_semaphore()

    def greet(device):
        pl.semaphore_signal(barrier, inc=1, device_id=device, device_id_type=MESH)

    for k in range(1, 4):
        greet((dp, 4 * m + lax.rem(q + k, 4)))
    for k in range(1, NX):
        greet(dev(y, zh, lax.rem(x + k, NX), space))

    @pl.when(m > 0)
    def _():
        greet((dp, 4 * m - 1))

    @pl.when(m < 2)
    def _():
        greet((dp, 4 * m + 4))

    for k in range(NY):
        @pl.when(jnp.logical_and(active, jnp.logical_or(share != home, y != k)))
        def _():
            greet(dev(k, zh, x, zl * 2 + lax.div(y, 4)))

    z_mine = jnp.logical_and(active, core == zh)
    slot = zh * 3 + m
    for j in range(NSRC):
        @pl.when(jnp.logical_not(jnp.logical_and(z_mine, slot == j)))
        def _():
            greet(dev(y, j // 3, x, (2 * (j % 3) + lax.rem(home, 2)) * 2 + zh))

    lower = jnp.logical_and(q == 0, m > 0)
    upper = jnp.logical_and(q == 3, m < 2)
    edge = jnp.logical_or(lower, upper)
    expected = (
        3 + jnp.where(edge, 4, 0) + 3 + (4 - jnp.where(share == home, 1, 0))
        + jnp.where(active, 12 - jnp.where(core == zh, 1, 0), 0)
    )

    column = lax.rem(lax.broadcasted_iota(jnp.int32, (PIX, COUT), 0), COLS)
    has_left = column >= SHIFT
    has_right = column < COLS - SHIFT

    def from_left(v):
        return jnp.where(has_left, pltpu.roll(v, SHIFT, 0), 0.0)

    def from_right(v):
        return jnp.where(has_right, pltpu.roll(v, PIX - SHIFT, 0), 0.0)

    def gather_taps(p):
        return p[:, COUT : 2 * COUT] + from_left(p[:, :COUT]) + from_right(p[:, 2 * COUT : 3 * COUT])

    def products(rows):
        w = jnp.concatenate([wv[3 * a + b] for a in rows for b in range(3)], axis=1)
        return jnp.dot(fv[...], w, preferred_element_type=F32)

    @pl.when(space == 0)
    def _():
        rq[0] = jnp.zeros((PIX, COUT), F32)
        gs[1, pl.ds(0, PIX)] = jnp.zeros((PIX, COUT), BF16)

    @pl.when(space == BANDS - 1)
    def _():
        rq[1] = jnp.zeros((PIX, COUT), F32)

    @pl.when(jnp.logical_and(m == 0, space != 0))
    def _():
        gs[1, pl.ds(0, PIX)] = jnp.zeros((PIX, COUT), BF16)

    @pl.when(m == 2)
    def _():
        gs[1, pl.ds(5 * PIX, PIX)] = jnp.zeros((PIX, COUT), BF16)

    cwp[...] = jnp.zeros((COUT, COUT), F32)
    pz[pl.ds(144, 16), :] = jnp.zeros((16, COUT), F32)

    loads[0].wait()
    loads[1].wait()
    loads[2].wait()
    both = products((0, 2))
    qs[0] = gather_taps(both[:, : 3 * COUT])
    qs[1] = gather_taps(both[:, 3 * COUT :])
    pl.semaphore_wait(barrier, expected)

    up = send(qs.at[0], rq.at[0], qs_sem.at[0], rq_sem.at[0], (dp, lax.rem(space + 1, BANDS)))
    down = send(qs.at[1], rq.at[1], qs_sem.at[1], rq_sem.at[1], (dp, lax.rem(space + BANDS - 1, BANDS)))

    @pl.when(space < BANDS - 1)
    def _():
        up.start()

    @pl.when(space > 0)
    def _():
        down.start()

    def band_of(k):
        return pl.ds(k * PIX, PIX)

    def quarter_copy(k):
        return send(
            fv.at[:, pl.ds((2 * (k % 2) + k // 2) * QUARTER, QUARTER)],
            quarter.at[pl.ds(pl.multiple_of(q * PIX, PIX), PIX)],
            fs_sem.at[k], fr_sem.at[q], (dp, 4 * m + k))

    for k in range(4):
        @pl.when(q != k)
        def _():
            quarter_copy(k).start()

        @pl.when(q == k)
        def _():
            pltpu.make_async_copy(
                fv.at[:, pl.ds((2 * (k % 2) + k // 2) * QUARTER, QUARTER)],
                quarter.at[band_of(k)], fr_sem.at[q]).start()

    loads[3].wait()
    for c in small:
        c.wait()
    cwp[pl.ds(0, NCLS), :] = cwt_ref[...].astype(F32)
    local = gather_taps(products((1,))) + bias_ref[...]

    eye = (
        lax.broadcasted_iota(jnp.int32, (COLS, COLS), 0)
        == lax.broadcasted_iota(jnp.int32, (COLS, COLS), 1)
    )

    def per_pixel(ref):
        return jnp.concatenate(
            [
                jnp.sum(
                    jnp.where(eye, jnp.broadcast_to(ref[r].astype(F32), (COLS, COLS)), 0.0),
                    axis=1, keepdims=True,
                )
                for r in range(ROWS)
            ],
            axis=0,
        )

    label = per_pixel(lab_ref)
    weight = per_pixel(pw_ref)

    @pl.when(space > 0)
    def _():
        up.wait_recv()

    @pl.when(space < BANDS - 1)
    def _():
        down.wait_recv()

    preact = local + rq[0] + rq[1]
    sig = jax.nn.sigmoid(preact)
    hidden = (preact * sig).astype(BF16)
    proj = cwp[...]
    logits = lax.dot_general(
        hidden, proj.astype(BF16), (((1,), (1,)), ((), ())), preferred_element_type=F32)
    lane = lax.broadcasted_iota(jnp.int32, (PIX, COUT), 1)
    real = lane < NCLS
    expo = jnp.where(real, jnp.exp(logits), 0.0)
    chances = expo / jnp.sum(expo, axis=1, keepdims=True)
    onehot = jnp.where(lane.astype(F32) == label, 1.0, 0.0)
    grad_logits = jnp.where(real, weight * (chances - onehot), 0.0)
    hidden_grad = lax.dot_general(
        grad_logits, proj, (((1,), (0,)), ((), ())),
        precision=lax.Precision.HIGHEST, preferred_element_type=F32)
    grad = hidden_grad * sig * (1.0 + preact * (1.0 - sig))

    def window(w):
        return pl.ds(pl.multiple_of(w * PIX, PIX), PIX)

    mine = window(q + 1)
    gs[1, mine] = grad.astype(BF16)
    for k in range(1, 4):
        send(gs.at[1, mine], gs.at[1, mine], gs_sem.at[k - 1], gr_sem.at[q + 1],
             (dp, 4 * m + lax.rem(q + k, 4))).start()

    def halo_copy(k):
        return send(
            gs.at[1, mine], gs.at[1, window(jnp.where(q == 0, 5, 0))],
            gh_sem.at[k], gr_sem.at[jnp.where(q == 0, 5, 0)],
            (dp, lax.rem(4 * (m + jnp.where(q == 0, 2, 1)), BANDS) + k))

    @pl.when(edge)
    def _():
        for k in range(4):
            halo_copy(k).start()

    def spread(w):
        g = gs[1, window(w)].astype(F32)
        gs[0, window(w)] = from_right(g).astype(BF16)
        gs[2, window(w)] = from_left(g).astype(BF16)

    spread(q + 1)
    for k in range(4):
        arrived(quarter.at[band_of(k)], fr_sem.at[k])
    columns = quarter[...].T
    for k in range(1, 4):
        w = 1 + lax.rem(q + k, 4)
        arrived(gs.at[1, window(w)], gr_sem.at[w])
        spread(w)

    def x_copy(a, k):
        to = lax.rem(x + k, NX)
        return send(
            con.at[a, to], rx.at[a, k - 1], xs_sem.at[a, k - 1], xr_sem.at[a, k - 1],
            dev(y, zh, to, space))

    def contribute(a):
        rhs = jnp.concatenate(
            [gs[b, pl.ds((2 - a) * PIX, 4 * PIX)] for b in range(3)], axis=1)
        total = jnp.dot(columns, rhs, preferred_element_type=F32).astype(BF16)
        for n in range(QUARTER // 16):
            yz, xd = divmod(n, NX)
            for b in range(3):
                con[a, xd, pl.ds((yz * 3 + b) * 16, 16), :] = total[
                    n * 16 : (n + 1) * 16, b * COUT : (b + 1) * COUT]
        for k in (2, 1, 3):
            x_copy(a, k).start()

    contribute(1)

    @pl.when(m < 2)
    def _():
        arrived(gs.at[1, window(5)], gr_sem.at[5])

    spread(5)
    contribute(0)

    @pl.when(m > 0)
    def _():
        arrived(gs.at[1, window(0)], gr_sem.at[0])

    spread(0)
    contribute(2)

    around = jnp.concatenate(
        [gs[b, window(q + 2 - a)] for a in range(3) for b in range(3)], axis=1)
    outs = []
    for n in range(4):
        width = CIN // 4
        wn = jnp.concatenate([wv[t, pl.ds(n * width, width)] for t in range(9)], axis=1)
        fg[:, pl.ds(n * width, width)] = lax.dot_general(
            around, wn, (((1,), (1,)), ((), ())), preferred_element_type=F32)
        outs.append(
            pltpu.make_async_copy(
                fg.at[:, pl.ds(n * width, width)], fg_hbm.at[:, pl.ds(n * width, width)],
                out_sem.at[n]))
        outs[-1].start()

    def y_target(yz):
        return dev(2 * share + yz // 2, zh, x, zl * 2 + yz % 2)

    def y_copy(a, yz):
        return send(
            cy.at[a, pl.ds(yz * 48, 48)], ry.at[a, y], ys_sem.at[a, yz], yr_sem.at[a, y],
            y_target(yz))

    def y_is_self(yz):
        return jnp.logical_and(y == 2 * share + yz // 2, core == yz % 2)

    for a in (1, 0, 2):
        for k in (2, 1, 3):
            x_copy(a, k).wait_recv()
        total = con[a, x].astype(F32)
        for k in range(3):
            total = total + rx[a, k].astype(F32)
        cy[a] = total.astype(BF16)
        for yz in range(4):
            itself = y_is_self(yz)

            @pl.when(itself)
            def _():
                pltpu.make_async_copy(
                    cy.at[a, pl.ds(yz * 48, 48)], ry.at[a, y], yr_sem.at[a, y]).start()

            @pl.when(jnp.logical_not(itself))
            def _():
                y_copy(a, yz).start()

    def z_copy(s):
        return send(cz.at[s], rz.at[slot], zs_sem.at[s], zr_sem.at[slot], dev(y, core, x, s))

    def z_is_self(s):
        return jnp.logical_and(core == zh, space == s)

    @pl.when(active)
    def _():
        for a in (1, 0, 2):
            total = None
            for k in range(NY):
                arrived(ry.at[a, k], yr_sem.at[a, k])
                part = ry[a, k].astype(F32)
                total = part if total is None else total + part
            for b in range(3):
                pz[pl.ds(3 * a + b, 16, stride=9), :] = total[b * 16 : (b + 1) * 16]
        for s in range(BANDS):
            cz[s] = pz[pl.ds(12 * s, 16), :].astype(BF16)
        for s in range(BANDS):
            @pl.when(z_is_self(s))
            def _():
                pltpu.make_async_copy(cz.at[s], rz.at[slot], zr_sem.at[slot]).start()

            @pl.when(jnp.logical_not(z_is_self(s)))
            def _():
                z_copy(s).start()

    for c in outs:
        c.wait()

    @pl.when(space < BANDS - 1)
    def _():
        up.wait_send()

    @pl.when(space > 0)
    def _():
        down.wait_send()

    for k in range(4):
        @pl.when(q != k)
        def _():
            quarter_copy(k).wait_send()

    for k in range(1, 4):
        send(gs.at[1, mine], gs.at[1, mine], gs_sem.at[k - 1], gr_sem.at[q + 1],
             (dp, 4 * m + lax.rem(q + k, 4))).wait_send()

    @pl.when(edge)
    def _():
        for k in range(4):
            halo_copy(k).wait_send()

    for a in range(3):
        for k in range(1, NX):
            x_copy(a, k).wait_send()
        for yz in range(4):
            @pl.when(jnp.logical_not(y_is_self(yz)))
            def _():
                y_copy(a, yz).wait_send()

    @pl.when(active)
    def _():
        for s in range(BANDS):
            @pl.when(jnp.logical_not(z_is_self(s)))
            def _():
                z_copy(s).wait_send()

    for j in range(NSRC):
        arrived(rz.at[j], zr_sem.at[j])


def write_kernel(fg_in, rz_in, fg_out, wg_out, fg, rz, wg, in_sem, out_sem):
    parts = WRITES
    rows = PIX // parts
    first = pltpu.make_async_copy(rz_in, rz, in_sem.at[parts])
    first.start()
    copies = []
    for n in range(parts):
        at = pl.ds(n * rows, rows)
        copies.append((
            pltpu.make_async_copy(fg_in.at[at], fg.at[at], in_sem.at[n]),
            pltpu.make_async_copy(fg.at[at], fg_out.at[at], out_sem.at[n]),
        ))
        copies[-1][0].start()
    first.wait()
    total = rz[0].astype(F32)
    for j in range(1, NSRC):
        total = total + rz[j].astype(F32)
    wg[...] = total[:12] / IMAGES
    last = pltpu.make_async_copy(wg, wg_out, out_sem.at[parts])
    last.start()
    for load, store in copies:
        load.wait()
        store.start()
    for load, store in copies:
        store.wait()
    last.wait()


def on_device(features, labels, pixel_weight, conv_weight, conv_bias, class_weight):
    image = features.reshape(PIX, CIN)
    taps = conv_weight.transpose(1, 0, 2)
    hbm = pl.BlockSpec(memory_space=pltpu.HBM)
    dma = pltpu.SemaphoreType.DMA
    feature_grad, pieces = pl.pallas_call(
        step_kernel,
        out_shape=(
            jax.ShapeDtypeStruct((PIX, CIN), F32),
            jax.ShapeDtypeStruct((NSRC, 16, COUT), BF16),
        ),
        in_specs=[hbm] * 6,
        out_specs=(hbm, hbm),
        scratch_shapes=[
            pltpu.VMEM((PIX, CIN), BF16),
            pltpu.VMEM((9, CIN, COUT), BF16),
            pltpu.VMEM((ROWS, 1, COLS), jnp.int32),
            pltpu.VMEM((ROWS, 1, COLS), jnp.int32),
            pltpu.VMEM((1, COUT), F32),
            pltpu.VMEM((NCLS, COUT), BF16),
            pltpu.VMEM((4 * PIX, QUARTER), BF16),
            pltpu.VMEM((COUT, COUT), F32),
            pltpu.VMEM((2, PIX, COUT), F32),
            pltpu.VMEM((2, PIX, COUT), F32),
            pltpu.VMEM((3, 6 * PIX, COUT), BF16),
            pltpu.VMEM((3, NX, 192, COUT), BF16),
            pltpu.VMEM((3, NX - 1, 192, COUT), BF16),
            pltpu.VMEM((3, 192, COUT), BF16),
            pltpu.VMEM((3, NY, 48, COUT), BF16),
            pltpu.VMEM((160, COUT), F32),
            pltpu.VMEM((BANDS, 16, COUT), BF16),
            pltpu.VMEM((PIX, CIN), F32),
            dma((8,)), dma((4,)), dma((2,)), dma((2,)), dma((4,)), dma((4,)), dma((3,)), dma((4,)), dma((6,)),
            dma((3, 3)), dma((3, 3)), dma((3, 4)), dma((3, NY)), dma((BANDS,)), dma((NSRC,)),
        ],
        compiler_params=pltpu.CompilerParams(
            collective_id=0, has_side_effects=True, vmem_limit_bytes=VMEM_LIMIT),
        name="step",
    )(
        image, taps, labels.transpose(1, 0, 2), pixel_weight.transpose(1, 0, 2),
        conv_bias.reshape(1, COUT), class_weight.T,
    )
    feature_grad, weight_grad = pl.pallas_call(
        write_kernel,
        out_shape=(
            jax.ShapeDtypeStruct((PIX, CIN), F32),
            jax.ShapeDtypeStruct((12, COUT), F32),
        ),
        in_specs=[hbm] * 2,
        out_specs=(hbm, hbm),
        scratch_shapes=[
            pltpu.VMEM((PIX, CIN), F32),
            pltpu.VMEM((NSRC, 16, COUT), BF16),
            pltpu.VMEM((12, COUT), F32),
            dma((WRITES + 1,)), dma((WRITES + 1,)),
        ],
        compiler_params=pltpu.CompilerParams(vmem_limit_bytes=VMEM_LIMIT),
        name="write",
    )(feature_grad, pieces)
    return feature_grad.reshape(features.shape), weight_grad


def solution(mesh):
    placed = (
        P("dp", "space", None, None),
        P("dp", "space", None),
        P("dp", "space", None),
        P(),
        P(),
        P(),
    )
    return jax.shard_map(
        on_device,
        mesh=mesh,
        in_specs=placed,
        out_specs=(P("dp", "space", None, None), P(("dp", "space"), None)),
        check_vma=False,
    )
```

time: 58.4 us -> 52.4 us (0.90)
  local copies, waits for them, and re-layouts: 3.38 us -> 0 us
  Pallas kernels: 54.1 us -> 51.6 us
    pallas_call x1, Pallas kernels: 54.1 us -> 49.5 us  [on_device(): pl.pallas_call(step_kernel, out_shape=(jax.ShapeDtypeStruct((PIX, CIN), F...]
    unnamed x2 -> x0, local copies, waits for them, and re-layouts: 3.38 us -> none
    pallas_call x0 -> x1, Pallas kernels: none -> 2.03 us  [on_device(): pl.pallas_call(write_kernel, out_shape=(jax.ShapeDtypeStruct((PIX, CIN),...]
where the time goes in v2:
time: 52.4 us; the launch traced here: 52.2 us
  Pallas kernels  51.6 us (98%)
  between operations  0.64 us (1%)
    pallas_call x1, Pallas kernels, on_device(): pl.pallas_call(step_kernel, out_shape=(jax.ShapeDtypeStruct((PIX, CIN), F...  49.5 us
    pallas_call x1, Pallas kernels, on_device(): pl.pallas_call(write_kernel, out_shape=(jax.ShapeDtypeStruct((PIX, CIN),...  2.03 us

profile of v2, /device:TPU:1, one launch (start us, length us, event | category | flops | bytes accessed | tf_op | source)
XLA Modules:
  0.0 52.2 jit_solution(4665738271328475233)
XLA Ops:
  0.6 49.5 %step.1 = (f32[192,1024]{1,0:T(8,128)}, bf16[6,16,128]{2,1,0:T(8,128)(2,1)}) custom-call(bf16[192,1024]{1,0:T(8,128)(2,1)} %bitcast.8, bf16[9,1024,128]{2,1,0:T(8,128)(2,1)} %bitcast.7, s32[6,1,32]{2,1,0:T(1,128)} %bitcast.9, s32[6,1,32]{2,1,0:T(1,128)} %bitcast.10, f32[1,128]{1,0:T(1,128)} %bitcast.12, bf16[3,128]{1,0:T(4,128)(2,1)} %bitcast.11), custom_call_target="tpu_custom_call" | custom-call | tf_op jit(solution)/shard_map/step/pallas_call | solution.py:449
  50.2 2.0 %write.1 = (f32[192,1024]{1,0:T(8,128)}, f32[12,128]{1,0:T(8,128)}) custom-call(f32[192,1024]{1,0:T(8,128)} %get-tuple-element.6.fg_in, bf16[6,16,128]{2,1,0:T(8,128)(2,1)} %get-tuple-element.7.rz_in), custom_call_target="tpu_custom_call" | custom-call | tf_op jit(solution)/shard_map/write/pallas_call | solution.py:486

commit v3 on v2

--- a/solution.py
+++ b/solution.py
@@ -25,9 +25,9 @@
     f_hbm, w_hbm, lab_hbm, pw_hbm, bias_hbm, cwt_hbm,
     fg_hbm, rz,
     fv, wv, lab_ref, pw_ref, bias_ref, cwt_ref,
-    quarter, cwp, qs, rq, gs, con, rx, cy, ry, pz, cz, fg,
+    quarter, cwp, qs, rq, gs, con, rx, cy, ry, con1, rx1, cy1, ry1, early, early_in, late, late_in, pz, cz, fg,
     load_sem, out_sem, qs_sem, rq_sem, fs_sem, fr_sem, gs_sem, gh_sem, gr_sem,
-    xs_sem, xr_sem, ys_sem, yr_sem, zs_sem, zr_sem,
+    xs_sem, xr_sem, ys_sem, yr_sem, es_sem, er_sem, ls_sem, lr_sem, zs_sem, zr_sem,
 ):
     dp = lax.axis_index("dp")
     space = lax.axis_index("space")
@@ -264,23 +264,57 @@
         arrived(gs.at[1, window(w)], gr_sem.at[w])
         spread(w)
 
-    def x_copy(a, k):
+    def group(n, wide, narrow):
+        return narrow if n == 0 else wide.at[n - 1]
+
+    def group_rows(n):
+        return 16 if n == 0 else 48
+
+    def x_copy(n, k):
         to = lax.rem(x + k, NX)
         return send(
-            con.at[a, to], rx.at[a, k - 1], xs_sem.at[a, k - 1], xr_sem.at[a, k - 1],
-            dev(y, zh, to, space))
+            group(n, con, con1).at[to], group(n, rx, rx1).at[k - 1],
+            xs_sem.at[n, k - 1], xr_sem.at[n, k - 1], dev(y, zh, to, space))
+
+    def y_target(yz):
+        return dev(2 * share + yz // 2, zh, x, zl * 2 + yz % 2)
+
+    def y_is_self(yz):
+        return jnp.logical_and(y == 2 * share + yz // 2, core == yz % 2)
+
+    def y_send(src, dst, send_sem, recv_sem, yz):
+        itself = y_is_self(yz)
+
+        @pl.when(itself)
+        def _():
+            pltpu.make_async_copy(src, dst, recv_sem).start()
+
+        @pl.when(jnp.logical_not(itself))
+        def _():
+            send(src, dst, send_sem, recv_sem, y_target(yz)).start()
+
+    def early_refs(yz):
+        return early.at[yz], early_in.at[y], es_sem.at[yz], er_sem.at[y]
 
     def contribute(a):
         rhs = jnp.concatenate(
             [gs[b, pl.ds((2 - a) * PIX, 4 * PIX)] for b in range(3)], axis=1)
         total = jnp.dot(columns, rhs, preferred_element_type=F32).astype(BF16)
-        for n in range(QUARTER // 16):
-            yz, xd = divmod(n, NX)
+        for c in range(QUARTER // 16):
+            yz, xd = divmod(c, NX)
             for b in range(3):
-                con[a, xd, pl.ds((yz * 3 + b) * 16, 16), :] = total[
-                    n * 16 : (n + 1) * 16, b * COUT : (b + 1) * COUT]
+                piece = total[c * 16 : (c + 1) * 16, b * COUT : (b + 1) * COUT]
+                if a != 1:
+                    con[a // 2, xd, pl.ds((yz * 3 + b) * 16, 16), :] = piece
+                elif b == 0:
+                    con1[xd, pl.ds(yz * 16, 16), :] = piece
+                else:
+                    early[yz, pl.ds((xd * 2 + b - 1) * 16, 16), :] = piece
         for k in (2, 1, 3):
-            x_copy(a, k).start()
+            x_copy((1, 0, 2)[a], k).start()
+        if a == 1:
+            for yz in range(4):
+                y_send(*early_refs(yz), yz)
 
     contribute(1)
 
@@ -312,35 +346,27 @@
                 out_sem.at[n]))
         outs[-1].start()
 
-    def y_target(yz):
-        return dev(2 * share + yz // 2, zh, x, zl * 2 + yz % 2)
-
-    def y_copy(a, yz):
+    def y_refs(n, yz):
+        rows = group_rows(n)
+        return (
+            group(n, cy, cy1).at[pl.ds(yz * rows, rows)], group(n, ry, ry1).at[y],
+            ys_sem.at[n, yz], yr_sem.at[n, y])
+
+    for n in range(3):
+        for k in (2, 1, 3):
+            x_copy(n, k).wait_recv()
+        total = group(n, con, con1)[x].astype(F32)
+        for k in range(3):
+            total = total + group(n, rx, rx1)[k].astype(F32)
+        group(n, cy, cy1)[...] = total.astype(BF16)
+        for yz in range(4):
+            y_send(*y_refs(n, yz), yz)
+
+    def late_copy(k):
+        to = lax.rem(x + k, NX)
         return send(
-            cy.at[a, pl.ds(yz * 48, 48)], ry.at[a, y], ys_sem.at[a, yz], yr_sem.at[a, y],
-            y_target(yz))
-
-    def y_is_self(yz):
-        return jnp.logical_and(y == 2 * share + yz // 2, core == yz % 2)
-
-    for a in (1, 0, 2):
-        for k in (2, 1, 3):
-            x_copy(a, k).wait_recv()
-        total = con[a, x].astype(F32)
-        for k in range(3):
-            total = total + rx[a, k].astype(F32)
-        cy[a] = total.astype(BF16)
-        for yz in range(4):
-            itself = y_is_self(yz)
-
-            @pl.when(itself)
-            def _():
-                pltpu.make_async_copy(
-                    cy.at[a, pl.ds(yz * 48, 48)], ry.at[a, y], yr_sem.at[a, y]).start()
-
-            @pl.when(jnp.logical_not(itself))
-            def _():
-                y_copy(a, yz).start()
+            late.at[to], late_in.at[k - 1], ls_sem.at[k - 1], lr_sem.at[k - 1],
+            dev(y, zh, to, space))
 
     def z_copy(s):
         return send(cz.at[s], rz.at[slot], zs_sem.at[s], zr_sem.at[slot], dev(y, core, x, s))
@@ -350,14 +376,29 @@
 
     @pl.when(active)
     def _():
-        for a in (1, 0, 2):
+        total = None
+        for k in range(NY):
+            arrived(early_in.at[k], er_sem.at[k])
+            part = early_in[k].astype(F32)
+            total = part if total is None else total + part
+        for to in range(NX):
+            late[to] = total[to * 32 : (to + 1) * 32].astype(BF16)
+        for k in (2, 1, 3):
+            late_copy(k).start()
+        for n in range(3):
             total = None
             for k in range(NY):
-                arrived(ry.at[a, k], yr_sem.at[a, k])
-                part = ry[a, k].astype(F32)
+                arrived(group(n, ry, ry1).at[k], yr_sem.at[n, k])
+                part = group(n, ry, ry1)[k].astype(F32)
                 total = part if total is None else total + part
-            for b in range(3):
-                pz[pl.ds(3 * a + b, 16, stride=9), :] = total[b * 16 : (b + 1) * 16]
+            for b, tap in enumerate(((3,), (0, 1, 2), (6, 7, 8))[n]):
+                pz[pl.ds(tap, 16, stride=9), :] = total[b * 16 : (b + 1) * 16]
+        total = late[x].astype(F32)
+        for k in (2, 1, 3):
+            late_copy(k).wait_recv()
+            total = total + late_in[k - 1].astype(F32)
+        for b in range(2):
+            pz[pl.ds(4 + b, 16, stride=9), :] = total[b * 16 : (b + 1) * 16]
         for s in range(BANDS):
             cz[s] = pz[pl.ds(12 * s, 16), :].astype(BF16)
         for s in range(BANDS):
@@ -394,16 +435,20 @@
         for k in range(4):
             halo_copy(k).wait_send()
 
-    for a in range(3):
+    for n in range(3):
         for k in range(1, NX):
-            x_copy(a, k).wait_send()
-        for yz in range(4):
-            @pl.when(jnp.logical_not(y_is_self(yz)))
-            def _():
-                y_copy(a, yz).wait_send()
+            x_copy(n, k).wait_send()
+    for yz in range(4):
+        @pl.when(jnp.logical_not(y_is_self(yz)))
+        def _():
+            send(*early_refs(yz), y_target(yz)).wait_send()
+            for n in range(3):
+                send(*y_refs(n, yz), y_target(yz)).wait_send()
 
     @pl.when(active)
     def _():
+        for k in range(1, NX):
+            late_copy(k).wait_send()
         for s in range(BANDS):
             @pl.when(jnp.logical_not(z_is_self(s)))
             def _():
@@ -466,15 +511,24 @@
             pltpu.VMEM((2, PIX, COUT), F32),
             pltpu.VMEM((2, PIX, COUT), F32),
             pltpu.VMEM((3, 6 * PIX, COUT), BF16),
-            pltpu.VMEM((3, NX, 192, COUT), BF16),
-            pltpu.VMEM((3, NX - 1, 192, COUT), BF16),
-            pltpu.VMEM((3, 192, COUT), BF16),
-            pltpu.VMEM((3, NY, 48, COUT), BF16),
+            pltpu.VMEM((2, NX, 192, COUT), BF16),
+            pltpu.VMEM((2, NX - 1, 192, COUT), BF16),
+            pltpu.VMEM((2, 192, COUT), BF16),
+            pltpu.VMEM((2, NY, 48, COUT), BF16),
+            pltpu.VMEM((NX, 64, COUT), BF16),
+            pltpu.VMEM((NX - 1, 64, COUT), BF16),
+            pltpu.VMEM((64, COUT), BF16),
+            pltpu.VMEM((NY, 16, COUT), BF16),
+            pltpu.VMEM((4, 128, COUT), BF16),
+            pltpu.VMEM((NY, 128, COUT), BF16),
+            pltpu.VMEM((NX, 32, COUT), BF16),
+            pltpu.VMEM((NX - 1, 32, COUT), BF16),
             pltpu.VMEM((160, COUT), F32),
             pltpu.VMEM((BANDS, 16, COUT), BF16),
             pltpu.VMEM((PIX, CIN), F32),
             dma((8,)), dma((4,)), dma((2,)), dma((2,)), dma((4,)), dma((4,)), dma((3,)), dma((4,)), dma((6,)),
-            dma((3, 3)), dma((3, 3)), dma((3, 4)), dma((3, NY)), dma((BANDS,)), dma((NSRC,)),
+            dma((3, 3)), dma((3, 3)), dma((3, 4)), dma((3, NY)),
+            dma((4,)), dma((NY,)), dma((3,)), dma((3,)), dma((BANDS,)), dma((NSRC,)),
         ],
         compiler_params=pltpu.CompilerParams(
             collective_id=0, has_side_effects=True, vmem_limit_bytes=VMEM_LIMIT),

time: 52.4 us -> 51.2 us (0.977)
  Pallas kernels: 51.6 us -> 50.4 us
    pallas_call x1, Pallas kernels: 49.5 us -> 48.3 us  [on_device(): pl.pallas_call(step_kernel, out_shape=(jax.ShapeDtypeStruct((PIX, CIN), F...]
where the time goes in v3:
time: 51.2 us; the launch traced here: 51 us
  Pallas kernels  50.4 us (98%)
  between operations  0.64 us (1%)
    pallas_call x1, Pallas kernels, on_device(): pl.pallas_call(step_kernel, out_shape=(jax.ShapeDtypeStruct((PIX, CIN), F...  48.3 us
    pallas_call x1, Pallas kernels, on_device(): pl.pallas_call(write_kernel, out_shape=(jax.ShapeDtypeStruct((PIX, CIN),...  2.03 us

profile of v3, /device:TPU:1, one launch (start us, length us, event | category | flops | bytes accessed | tf_op | source)
XLA Modules:
  0.0 51.0 jit_solution(8988254628994393047)
XLA Ops:
  0.6 48.3 %step.1 = (f32[192,1024]{1,0:T(8,128)}, bf16[6,16,128]{2,1,0:T(8,128)(2,1)}) custom-call(bf16[192,1024]{1,0:T(8,128)(2,1)} %bitcast.8, bf16[9,1024,128]{2,1,0:T(8,128)(2,1)} %bitcast.7, s32[6,1,32]{2,1,0:T(1,128)} %bitcast.9, s32[6,1,32]{2,1,0:T(1,128)} %bitcast.10, f32[1,128]{1,0:T(1,128)} %bitcast.12, bf16[3,128]{1,0:T(4,128)(2,1)} %bitcast.11), custom_call_target="tpu_custom_call" | custom-call | tf_op jit(solution)/shard_map/step/pallas_call | solution.py:494
  49.0 2.0 %write.1 = (f32[192,1024]{1,0:T(8,128)}, f32[12,128]{1,0:T(8,128)}) custom-call(f32[192,1024]{1,0:T(8,128)} %get-tuple-element.6.fg_in, bf16[6,16,128]{2,1,0:T(8,128)(2,1)} %get-tuple-element.7.rz_in), custom_call_target="tpu_custom_call" | custom-call | tf_op jit(solution)/shard_map/write/pallas_call | solution.py:540

commit v4 on v3

--- a/solution.py
+++ b/solution.py
@@ -235,19 +235,27 @@
 
     mine = window(q + 1)
     gs[1, mine] = grad.astype(BF16)
-    for k in range(1, 4):
-        send(gs.at[1, mine], gs.at[1, mine], gs_sem.at[k - 1], gr_sem.at[q + 1],
-             (dp, 4 * m + lax.rem(q + k, 4))).start()
+    partner = (dp, zl * 2 + 1 - core)
+
+    def across(k):
+        to = lax.rem(q + 2, 4) if k == 0 else 2 * lax.div(q, 2) + 1 - core
+        return send(gs.at[1, mine], gs.at[1, mine], gs_sem.at[k], gr_sem.at[q + 1], (dp, 4 * m + to))
+
+    def hand_on(k, w):
+        return send(gs.at[1, window(w)], gs.at[1, window(w)], gs_sem.at[2 + k], gr_sem.at[w], partner)
+
+    across(0).start()
+    across(1).start()
 
     def halo_copy(k):
         return send(
             gs.at[1, mine], gs.at[1, window(jnp.where(q == 0, 5, 0))],
             gh_sem.at[k], gr_sem.at[jnp.where(q == 0, 5, 0)],
-            (dp, lax.rem(4 * (m + jnp.where(q == 0, 2, 1)), BANDS) + k))
+            (dp, lax.rem(4 * (m + jnp.where(q == 0, 2, 1)), BANDS) + 2 * k + core))
 
     @pl.when(edge)
     def _():
-        for k in range(4):
+        for k in range(2):
             halo_copy(k).start()
 
     def spread(w):
@@ -259,10 +267,16 @@
     for k in range(4):
         arrived(quarter.at[band_of(k)], fr_sem.at[k])
     columns = quarter[...].T
-    for k in range(1, 4):
-        w = 1 + lax.rem(q + k, 4)
-        arrived(gs.at[1, window(w)], gr_sem.at[w])
-        spread(w)
+    opposite = 1 + lax.rem(q + 2, 4)
+    arrived(gs.at[1, window(opposite)], gr_sem.at[opposite])
+    hand_on(0, opposite).start()
+    spread(opposite)
+    beside = 1 + 2 * lax.div(q, 2) + 1 - core
+    arrived(gs.at[1, window(beside)], gr_sem.at[beside])
+    spread(beside)
+    last = 1 + lax.rem(beside + 1, 4)
+    arrived(gs.at[1, window(last)], gr_sem.at[last])
+    spread(last)
 
     def group(n, wide, narrow):
         return narrow if n == 0 else wide.at[n - 1]
@@ -322,12 +336,20 @@
     def _():
         arrived(gs.at[1, window(5)], gr_sem.at[5])
 
+    @pl.when(jnp.logical_and(m < 2, core == 0))
+    def _():
+        hand_on(1, 5).start()
+
     spread(5)
     contribute(0)
 
     @pl.when(m > 0)
     def _():
         arrived(gs.at[1, window(0)], gr_sem.at[0])
+
+    @pl.when(jnp.logical_and(m > 0, core == 1))
+    def _():
+        hand_on(1, 0).start()
 
     spread(0)
     contribute(2)
@@ -426,13 +448,21 @@
         def _():
             quarter_copy(k).wait_send()
 
-    for k in range(1, 4):
-        send(gs.at[1, mine], gs.at[1, mine], gs_sem.at[k - 1], gr_sem.at[q + 1],
-             (dp, 4 * m + lax.rem(q + k, 4))).wait_send()
+    across(0).wait_send()
+    across(1).wait_send()
+    hand_on(0, opposite).wait_send()
+
+    @pl.when(jnp.logical_and(m < 2, core == 0))
+    def _():
+        hand_on(1, 5).wait_send()
+
+    @pl.when(jnp.logical_and(m > 0, core == 1))
+    def _():
+        hand_on(1, 0).wait_send()
 
     @pl.when(edge)
     def _():
-        for k in range(4):
+        for k in range(2):
             halo_copy(k).wait_send()
 
     for n in range(3):
@@ -526,7 +556,7 @@
             pltpu.VMEM((160, COUT), F32),
             pltpu.VMEM((BANDS, 16, COUT), BF16),
             pltpu.VMEM((PIX, CIN), F32),
-            dma((8,)), dma((4,)), dma((2,)), dma((2,)), dma((4,)), dma((4,)), dma((3,)), dma((4,)), dma((6,)),
+            dma((8,)), dma((4,)), dma((2,)), dma((2,)), dma((4,)), dma((4,)), dma((4,)), dma((2,)), dma((6,)),
             dma((3, 3)), dma((3, 3)), dma((3, 4)), dma((3, NY)),
             dma((4,)), dma((NY,)), dma((3,)), dma((3,)), dma((BANDS,)), dma((NSRC,)),
         ],

time: 51.2 us -> 50.5 us (0.986)
  Pallas kernels: 50.4 us -> 49.7 us
    pallas_call x1, Pallas kernels: 48.3 us -> 47.7 us  [on_device(): pl.pallas_call(step_kernel, out_shape=(jax.ShapeDtypeStruct((PIX, CIN), F...]
where the time goes in v4:
time: 50.5 us; the launch traced here: 50.3 us
  Pallas kernels  49.7 us (98%)
  between operations  0.64 us (1%)
    pallas_call x1, Pallas kernels, on_device(): pl.pallas_call(step_kernel, out_shape=(jax.ShapeDtypeStruct((PIX, CIN), F...  47.7 us
    pallas_call x1, Pallas kernels, on_device(): pl.pallas_call(write_kernel, out_shape=(jax.ShapeDtypeStruct((PIX, CIN),...  2.03 us

profile of v4, /device:TPU:1, one launch (start us, length us, event | category | flops | bytes accessed | tf_op | source)
XLA Modules:
  0.0 50.3 jit_solution(853274044118455603)
XLA Ops:
  0.6 47.7 %step.1 = (f32[192,1024]{1,0:T(8,128)}, bf16[6,16,128]{2,1,0:T(8,128)(2,1)}) custom-call(bf16[192,1024]{1,0:T(8,128)(2,1)} %bitcast.8, bf16[9,1024,128]{2,1,0:T(8,128)(2,1)} %bitcast.7, s32[6,1,32]{2,1,0:T(1,128)} %bitcast.9, s32[6,1,32]{2,1,0:T(1,128)} %bitcast.10, f32[1,128]{1,0:T(1,128)} %bitcast.12, bf16[3,128]{1,0:T(4,128)(2,1)} %bitcast.11), custom_call_target="tpu_custom_call" | custom-call | tf_op jit(solution)/shard_map/step/pallas_call | solution.py:524
  48.3 2.0 %write.1 = (f32[192,1024]{1,0:T(8,128)}, f32[12,128]{1,0:T(8,128)}) custom-call(f32[192,1024]{1,0:T(8,128)} %get-tuple-element.6.fg_in, bf16[6,16,128]{2,1,0:T(8,128)(2,1)} %get-tuple-element.7.rz_in), custom_call_target="tpu_custom_call" | custom-call | tf_op jit(solution)/shard_map/write/pallas_call | solution.py:570

commit v5 on v4

--- a/solution.py
+++ b/solution.py
@@ -17,7 +17,7 @@
 BANDS = 12
 NSRC = 6
 IMAGES = 64
-WRITES = 8
+WRITES = 3
 VMEM_LIMIT = 60 * 1024 * 1024
 
 
@@ -324,11 +324,11 @@
                     con1[xd, pl.ds(yz * 16, 16), :] = piece
                 else:
                     early[yz, pl.ds((xd * 2 + b - 1) * 16, 16), :] = piece
-        for k in (2, 1, 3):
-            x_copy((1, 0, 2)[a], k).start()
         if a == 1:
             for yz in range(4):
                 y_send(*early_refs(yz), yz)
+        for k in (2, 1, 3):
+            x_copy((1, 0, 2)[a], k).start()
 
     contribute(1)
 

time: 50.5 us -> 50.3 us (level)
  no operation moved by 1% of the time
where the time goes in v5:
time: 50.3 us; the launch traced here: 50.2 us
  Pallas kernels  49.5 us (98%)
  between operations  0.64 us (1%)
    pallas_call x1, Pallas kernels, on_device(): pl.pallas_call(step_kernel, out_shape=(jax.ShapeDtypeStruct((PIX, CIN), F...  47.6 us
    pallas_call x1, Pallas kernels, on_device(): pl.pallas_call(write_kernel, out_shape=(jax.ShapeDtypeStruct((PIX, CIN),...  1.91 us

profile of v5, /device:TPU:1, one launch (start us, length us, event | category | flops | bytes accessed | tf_op | source)
XLA Modules:
  0.0 50.2 jit_solution(13467797933867027759)
XLA Ops:
  0.6 47.6 %step.1 = (f32[192,1024]{1,0:T(8,128)}, bf16[6,16,128]{2,1,0:T(8,128)(2,1)}) custom-call(bf16[192,1024]{1,0:T(8,128)(2,1)} %bitcast.8, bf16[9,1024,128]{2,1,0:T(8,128)(2,1)} %bitcast.7, s32[6,1,32]{2,1,0:T(1,128)} %bitcast.9, s32[6,1,32]{2,1,0:T(1,128)} %bitcast.10, f32[1,128]{1,0:T(1,128)} %bitcast.12, bf16[3,128]{1,0:T(4,128)(2,1)} %bitcast.11), custom_call_target="tpu_custom_call" | custom-call | tf_op jit(solution)/shard_map/step/pallas_call | solution.py:524
  48.3 1.9 %write.1 = (f32[192,1024]{1,0:T(8,128)}, f32[12,128]{1,0:T(8,128)}) custom-call(f32[192,1024]{1,0:T(8,128)} %get-tuple-element.6.fg_in, bf16[6,16,128]{2,1,0:T(8,128)(2,1)} %get-tuple-element.7.rz_in), custom_call_target="tpu_custom_call" | custom-call | tf_op jit(solution)/shard_map/write/pallas_call | solution.py:570
